TPU v7x, 256 devices: a whole 4x4x8 slice. The times are simulated.
256 devices in a mesh: head: 8 (over y, core), tok: 32 (over x, z).
Axes of the slice: x: 4, y: 4, z: 8, core: 2. Of those that a mesh axis runs over, the one named last changes fastest.
Arguments:
- hires_tokens: bfloat16 [131072, 1024], P('tok'), may hold values from -6 to 6
- lowres_tokens: bfloat16 [8192, 1024], P('tok'), may hold values from -6 to 6
- norm_gain: float32 [1024], replicated, may hold values from 0.1 to 1.9
- w_cross_q: bfloat16 [1024, 1024], P(None, 'head'), may hold values from -0.1875 to 0.1875
- w_low_kv: bfloat16 [1024, 2, 1024], P(None, None, 'head'), may hold values from -0.1875 to 0.1875
- w_view_qkv: bfloat16 [1024, 3, 1024], P(None, None, 'head'), may hold values from -0.1875 to 0.1875
- w_out: bfloat16 [2, 1024, 1024], P(None, 'head'), may hold values from -0.125 to 0.125
- block_lists: int32 [1024, 8], P('tok'), may hold values from 0 to 63, as said below
- block_counts: int32 [1024], P('tok'), may hold values from 1 to 8, as said below
Outputs:
- layer_out: bfloat16 [131072, 1024], P('tok', 'head')
Inputs may be any that keep to these rules, and one draw needn't show every extreme that they name: `block_lists`: each row names 8 distinct low-resolution blocks; only the first block_counts entries of a row are used. `block_counts`: in every draw there is at least one index of tok all of whose query blocks use all 8 entries; query blocks of the other indices may use any count from 1 to 8.
All inputs are finite; a program needn't handle non-finite values.
Results may differ from a plain program's by a relative error of at most 0.009.
Values may be sent and summed in bfloat16 or wider, within the bound.
A program may use at most 128 MiB of HBM per device.

v0:
```python
import math

import jax
import jax.numpy as jnp
from jax import lax
from jax.sharding import PartitionSpec as P

HD = 128
VIEWS = 8
BLOCK = 128
MAXB = 8


def rms_rows(row_block, norm_gain):
    values = row_block.astype(jnp.float32)
    factor = lax.rsqrt(jnp.mean(values * values, axis=-1, keepdims=True) + 1e-06)
    return (values * factor * norm_gain).astype(jnp.bfloat16)


def masked_softmax(scores, is_valid):
    exponent = jnp.where(is_valid, jnp.exp(scores), jnp.zeros_like(scores))
    return (exponent / jnp.sum(exponent, axis=-1, keepdims=True)).astype(jnp.bfloat16)


def shards(
    hires_tokens,
    lowres_tokens,
    norm_gain,
    w_cross_q,
    w_low_kv,
    w_view_qkv,
    w_out,
    block_lists,
    block_counts,
):
    tok_rows, model_width = hires_tokens.shape
    local_cols = w_cross_q.shape[1]
    heads_here = local_cols // HD
    normed = rms_rows(hires_tokens, norm_gain)
    low_normed = rms_rows(lowres_tokens, norm_gain)
    cross_query = jnp.dot(normed, w_cross_q, preferred_element_type=jnp.float32).astype(
        jnp.bfloat16
    )
    low_kv = jnp.dot(
        low_normed,
        w_low_kv.reshape(model_width, 2 * local_cols),
        preferred_element_type=jnp.float32,
    ).astype(jnp.bfloat16)
    all_kv = lax.all_gather(low_kv, "tok", axis=0, tiled=True)
    low_blocks = all_kv.reshape(-1, BLOCK, 2, heads_here, HD)
    q_blocks = tok_rows // BLOCK
    group_size = math.gcd(q_blocks, max(1, 512 // BLOCK))
    grouped_q = cross_query.reshape(q_blocks // group_size, group_size, BLOCK, heads_here, HD)
    grouped_ids = block_lists.reshape(q_blocks // group_size, group_size, MAXB)
    grouped_counts = block_counts.reshape(q_blocks // group_size, group_size)
    slot_of_key = jnp.arange(MAXB * BLOCK, dtype=jnp.int32) // BLOCK

    def attend_group(inputs):
        queries, block_ids, counts = inputs
        picked = low_blocks[block_ids].reshape(group_size, MAXB * BLOCK, 2, heads_here, HD)
        scores = jnp.einsum(
            "gqhe,gkhe->ghqk", queries, picked[:, :, 0], preferred_element_type=jnp.float32
        ) / math.sqrt(HD)
        is_valid = (slot_of_key[None, :] < counts[:, None])[:, None, None, :]
        weights = masked_softmax(scores, is_valid)
        mixed_out = jnp.einsum(
            "ghqk,gkhe->gqhe", weights, picked[:, :, 1], preferred_element_type=jnp.float32
        )
        return mixed_out.astype(jnp.bfloat16)

    cross_out = lax.map(attend_group, (grouped_q, grouped_ids, grouped_counts)).reshape(
        tok_rows, local_cols
    )
    view_qkv = jnp.dot(
        normed, w_view_qkv.reshape(model_width, 3 * local_cols), preferred_element_type=jnp.float32
    )
    view_qkv = view_qkv.astype(jnp.bfloat16).reshape(tok_rows, 3, local_cols)
    arrived = lax.all_to_all(view_qkv, "tok", split_axis=0, concat_axis=0, tiled=True)
    per_view = arrived.reshape(VIEWS, -1, 3, heads_here, HD)
    scores = jnp.einsum(
        "vphe,uphe->phvu", per_view[:, :, 0], per_view[:, :, 1], preferred_element_type=jnp.float32
    ) / math.sqrt(HD)
    weights = masked_softmax(scores, True)
    mixed_out = jnp.einsum(
        "phvu,uphe->vphe", weights, per_view[:, :, 2], preferred_element_type=jnp.float32
    )
    view_out = lax.all_to_all(
        mixed_out.astype(jnp.bfloat16).reshape(tok_rows, local_cols),
        "tok",
        split_axis=0,
        concat_axis=0,
        tiled=True,
    )
    partial_value = jnp.dot(cross_out, w_out[0], preferred_element_type=jnp.float32)
    partial_value = partial_value + jnp.dot(view_out, w_out[1], preferred_element_type=jnp.float32)
    summed = lax.psum_scatter(
        partial_value.astype(jnp.bfloat16), "head", scatter_dimension=1, tiled=True
    ).astype(jnp.float32)
    out_cols = summed.shape[1]
    residual = lax.dynamic_slice_in_dim(
        hires_tokens, lax.axis_index("head") * out_cols, out_cols, 1
    )
    return (residual.astype(jnp.float32) + summed).astype(jnp.bfloat16)


def solution(mesh):
    in_specs = (
        P("tok", None),
        P("tok", None),
        P(),
        P(None, "head"),
        P(None, None, "head"),
        P(None, None, "head"),
        P(None, "head", None),
        P("tok", None),
        P("tok"),
    )
    out_specs = P("tok", "head")
    return jax.shard_map(shards, mesh=mesh, in_specs=in_specs, out_specs=out_specs, check_vma=False)
```

profile of v0, /device:TPU:1, one launch (start us, length us, event | category | flops | bytes accessed | tf_op | source)
XLA Modules:
  0.0 336.0 jit_solution(16362410177113317148)
XLA Ops:
  6.5 1.3 fusion.21
  7.8 2.2 convolution_convert_fusion.4
  10.1 5.2 %fusion.15 = f32[4096]{0:T(1024)S(1)} fusion(bf16[4096,1024]{1,0:T(8,128)(2,1)} %param.11), kind=kLoop, calls=%fused_computation.31 | loop fusion | flops 12578816 | bytes 8404992 | tf_op jit(solution)/shard_map/reduce_sum | solution.py:16
  15.3 1.2 copy.49
  16.4 7.1 %convolution_convert_fusion.1 = bf16[4096,384]{0,1:T(8,128)(2,1)S(1)} fusion(bf16[1024,384]{0,1:T(8,128)(2,1)} %bitcast.92, bf16[4096,1024]{1,0:T(8,128)(2,1)} %param.11, f32[1024]{0:T(1024)S(1)} %copy-done.6, f32[4096]{0:T(1024)S(1)} %add_rsqrt_fusion), kind=kOutput, calls=%fused_computation.35 | convolution fusion | flops 3239575552 | bytes 12341248 | tf_op jit(solution)/shard_map/dot_general | solution.py:74
  23.5 4.8 %copy.50 = bf16[4096,3,128]{2,1,0:T(4,128)(2,1)} copy(bf16[4096,3,128]{0,2,1:T(8,128)(2,1)S(1)} %bitcast.89) | data formatting | bytes 6291456 | tf_op jit(solution)/shard_map/reshape | solution.py:77
  28.3 12.3 %all-to-all-start = ((bf16[4096,3,128]{2,1,0:T(4,128)(2,1)}), bf16[4096,3,128]{2,1,0:T(4,128)(2,1)}, u32[]{:S(2)}, u32[]{:S(2)}) async-start(bf16[4096,3,128]{2,1,0:T(4,128)(2,1)} %copy.50), calls=%async_computation | async-start | bytes 8388608 | tf_op jit(solution)/shard_map/all_to_all | solution.py:78
  40.7 6.9 %convolution_convert_fusion.2 = bf16[4096,128]{1,0:T(8,128)(2,1)} fusion(bf16[1024,128]{1,0:T(8,128)(2,1)S(1)} %copy-done, bf16[4096,1024]{1,0:T(8,128)(2,1)} %param.11, f32[1024]{0:T(1024)S(1)} %copy-done.6, f32[4096]{0:T(1024)S(1)} %add_rsqrt_fusion), kind=kOutput, calls=%fused_computation.36 | convolution fusion | flops 1091043328 | bytes 9719808 | tf_op jit(solution)/shard_map/dot_general | solution.py:41
  47.6 110.9 %all-to-all-done = bf16[4096,3,128]{2,1,0:T(4,128)(2,1)} async-done(((bf16[4096,3,128]{2,1,0:T(4,128)(2,1)}), bf16[4096,3,128]{2,1,0:T(4,128)(2,1)}, u32[]{:S(2)}, u32[]{:S(2)}) %all-to-all-start) | async-done | bytes 3145760 | tf_op jit(solution)/shard_map/all_to_all | solution.py:78
  158.6 2.6 copy.51
  161.4 1.3 fusion.24
  163.6 0.7 copy.56
  164.3 0.9 fusion.20
  165.2 1.2 copy.57
  166.3 4.6 %all-to-all-start.1 = ((bf16[32,128,128]{2,1,0:T(8,128)(2,1)}), bf16[32,128,128]{2,1,0:T(8,128)(2,1)S(1)}, u32[]{:S(2)}, u32[]{:S(2)}) async-start(bf16[32,128,128]{2,1,0:T(8,128)(2,1)} %bitcast.13), calls=%async_computation.1 | async-start | bytes 2097152 | tf_op jit(solution)/shard_map/all_to_all | solution.py:87
  171.2 7.0 %reshape.163 = bf16[64,128,2,1,128]{4,2,1,0,3:T(2,128)(2,1)} reshape(bf16[8192,256]{1,0:T(8,128)(2,1)} %all-gather.2.cloned.1.call-done) | data formatting | bytes 8388608 | tf_op jit(solution)/shard_map/reshape | solution.py:50
  178.2 5.3 %copy.46 = bf16[64,128,2,1,128]{4,1,3,2,0:T(8,128)(2,1)} copy(bf16[64,128,2,1,128]{4,2,1,0,3:T(2,128)(2,1)} %reshape.163) | data formatting | bytes 8388608
  183.5 53.3 %while.11 = (s32[]{:T(128)}, bf16[8,4,128,1,128]{4,2,1,0,3:T(8,128)(2,1)}, s32[8,4,8]{2,1,0:T(4,128)S(1)}, bf16[64,128,2,1,128]{4,1,3,2,0:T(8,128)(2,1)}, s32[8,...) while((s32[]{:T(128)}, bf16[8,4,128,1,128]{4,2,1,0,3:T(8,128)(2,1)}, ...), condition=%wide.region_4.5_spmd.clone, body=%wide.region_2.4_spmd.clone.sunk | while | flops 272183904 | bytes 15497093 | solution.py:71
  183.6 3.1 gather_fusion
  187.0 1.6 fusion.46
  188.5 0.8 fusion.47
  190.2 3.1 gather_fusion
  193.6 1.6 fusion.46
  195.2 0.8 fusion.47
  196.9 3.1 gather_fusion
  200.3 1.6 fusion.46
  201.9 0.8 fusion.47
  203.6 3.1 gather_fusion
  207.0 1.6 fusion.46
  208.5 0.8 fusion.47
  210.2 3.1 gather_fusion
  213.6 1.6 fusion.46
  215.2 0.8 fusion.47
  216.9 3.1 gather_fusion
  220.3 1.6 fusion.46
  221.9 0.8 fusion.47
  223.6 3.1 gather_fusion
  227.0 1.6 fusion.46
  228.5 0.8 fusion.47
  230.2 3.1 gather_fusion
  233.6 1.6 fusion.46
  235.2 0.8 fusion.47
  236.8 9.4 %fusion.31 = f32[4096,1024]{1,0:T(8,128)} fusion(bf16[4096,128]{1,0:T(8,128)(2,1)} %bitcast.90, bf16[2,128,1024]{2,1,0:T(8,128)(2,1)} %param.17), kind=kOutput, calls=%fused_computation.55 | convolution fusion | flops 1073741824 | bytes 18087936 | tf_op jit(solution)/shard_map/dot_general | solution.py:94
  246.2 11.3 %add_convert_fusion = bf16[4096,1024]{1,0:T(8,128)(2,1)} fusion(f32[4096,1024]{1,0:T(8,128)} %fusion.31, bf16[4096,128]{1,0:T(8,128)(2,1)S(1)} %bitcast.88, bf16[2,128,1024]{2,1,0:T(8,128)(2,1)S(1)} %copy-done.3), kind=kOutput, calls=%fused_computation.34 | convolution fusion | flops 1082130432 | bytes 26476544 | tf_op jit(solution)/shard_map/dot_general | solution.py:95
  257.5 11.3 %copy.59 = bf16[4096,1024]{0,1:T(8,128)(2,1)} copy(bf16[4096,1024]{1,0:T(8,128)(2,1)} %add_convert_fusion) | data formatting | bytes 16777216
  268.9 56.2 %reduce-scatter.4.cloned.1.call-done = bf16[128,4096]{1,0:T(8,128)(2,1)} async-done(((bf16[1024,4096]{1,0:T(8,128)(2,1)}), bf16[128,4096]{1,0:T(8,128)(2,1)}) %reduce-scatter.4.cloned.1.call-update) | async-done | bytes 1048592
  325.0 1.6 copy.60
  326.7 2.5 add_convert_fusion.1
  (101 shorter events, 10.6 us)
Async XLA Ops:
  6.5 34.2 %copy-start = (bf16[1024,128]{1,0:T(8,128)(2,1)S(1)}, bf16[1024,128]{1,0:T(8,128)(2,1)}, u32[]{:S(2)}) copy-start(bf16[1024,128]{1,0:T(8,128)(2,1)} %param.14) | copy-start | bytes 786436
  6.5 164.7 %all-gather.2.cloned.1.call-start = ((), (), s32[]{:S(2)}) async-start(), calls=%async_computation.3 | async-start | bytes 4325376 | tf_op jit(solution)/shard_map/all_gather | solution.py:49
  10.1 5.2 %copy-start.2 = (bf16[1024,3,128]{2,0,1:T(8,128)(2,1)S(1)}, bf16[1024,3,128]{2,0,1:T(8,128)(2,1)}, u32[]{:S(2)}) copy-start(bf16[1024,3,128]{2,0,1:T(8,128)(2,1)} %param.16) | copy-start | bytes 2359300
  10.1 6.4 %copy-start.6 = (f32[1024]{0:T(1024)S(1)}, f32[1024]{0:T(1024)}, u32[]{:S(2)}) copy-start(f32[1024]{0:T(1024)} %param.13) | copy-start | bytes 12292
  28.3 12.3 %copy-start.4 = (s32[32,8]{0,1:T(8,128)S(1)}, s32[32,8]{0,1:T(8,128)}, u32[]{:S(2)}) copy-start(s32[32,8]{0,1:T(8,128)} %param.18) | copy-start | bytes 3076
  28.3 12.4 %copy-start.5 = (s32[32]{0:T(128)S(1)}, s32[32]{0:T(128)}, u32[]{:S(2)}) copy-start(s32[32]{0:T(128)} %param.19) | copy-start | bytes 388
  28.3 130.3 %all-to-all-start = ((bf16[4096,3,128]{2,1,0:T(4,128)(2,1)}), bf16[4096,3,128]{2,1,0:T(4,128)(2,1)}, u32[]{:S(2)}, u32[]{:S(2)}) async-start(bf16[4096,3,128]{2,1,0:T(4,128)(2,1)} %copy.50), calls=%async_computation | async-start | bytes 8388608 | tf_op jit(solution)/shard_map/all_to_all | solution.py:78
  166.3 79.9 %all-to-all-start.1 = ((bf16[32,128,128]{2,1,0:T(8,128)(2,1)}), bf16[32,128,128]{2,1,0:T(8,128)(2,1)S(1)}, u32[]{:S(2)}, u32[]{:S(2)}) async-start(bf16[32,128,128]{2,1,0:T(8,128)(2,1)} %bitcast.13), calls=%async_computation.1 | async-start | bytes 2097152 | tf_op jit(solution)/shard_map/all_to_all | solution.py:87
  171.0 154.1 %reduce-scatter.4.cloned.1.call-start = ((), (), s32[]{:S(2)}) async-start(), calls=%async_computation.4 | async-start | bytes 9437184
  236.8 9.4 %copy-start.3 = (bf16[2,128,1024]{2,1,0:T(8,128)(2,1)S(1)}, bf16[2,128,1024]{2,1,0:T(8,128)(2,1)}, u32[]{:S(2)}) copy-start(bf16[2,128,1024]{2,1,0:T(8,128)(2,1)} %param.17) | copy-start | bytes 1572868
  268.8 60.3 %copy-start.1 = (bf16[1024,128]{1,0:T(8,128)(2,1)S(1)}, bf16[1024,128]{1,0:T(8,128)(2,1)}, u32[]{:S(2)}) copy-start(bf16[1024,128]{1,0:T(8,128)(2,1)} %param.14) | copy-start | bytes 786436
Sparse Core Ops, SparseCore 0:
  10.2 141.9 all-gather.1
  269.0 56.0 reduce-scatter.3
where the time goes:
time: 337 us; the launch traced here: 336 us
  waiting for transfers between devices  167 us (50%)
  local copies, waits for them, and re-layouts  70.1 us (21%)
  matrix products  57.9 us (17%)
  starting transfers between devices  17.2 us (5%)
  between operations  13.6 us (4%)
  other arithmetic  9.74 us (3%)
    all_to_all x1, waiting for transfers between devices, shards(): lax.all_to_all(view_qkv, 'tok', split_axis=0, concat_axis=0, tiled=True)  111 us
    unnamed x3, waiting for transfers between devices  56.2 us
    gather x16, local copies, waits for them, and re-layouts, attend_group(): low_blocks[block_ids].reshape(group_size, MAXB * BLOCK, 2, heads_here, HD)  26.2 us
    unnamed x19, local copies, waits for them, and re-layouts  19.5 us
    dot_general x8, matrix products, attend_group(): jnp.einsum('gqhe,gkhe->ghqk', queries, picked[:, :, 0], preferred_element...  12.6 us
    all_to_all x1, starting transfers between devices, shards(): lax.all_to_all(view_qkv, 'tok', split_axis=0, concat_axis=0, tiled=True)  12.3 us
    dot_general x1, matrix products, shards(): jnp.dot(view_out, w_out[1], preferred_element_type=jnp.float32)  11.3 us
    dot_general x1, matrix products, shards(): jnp.dot(cross_out, w_out[0], preferred_element_type=jnp.float32)  9.37 us
  transfers between devices with their start and end apart: 4, of which 2 were waited for; matrix products, arithmetic and copies ran while one was open for 32% of the time, Pallas kernels for 0%

commit v1 on v0

v1 whole, which is shorter than its diff:
```python
import functools
import math

import jax
import jax.numpy as jnp
from jax import lax
from jax.experimental import pallas as pl
from jax.experimental.pallas import tpu as pltpu
from jax.sharding import PartitionSpec as P

HD = 128
VIEWS = 8
MAXB = 8
NY, NZ = 4, 8
CH = 4
PIECE = 16
HEADS = 8
MASKED = -1e30
SCORE_SCALE = math.log2(math.e) / math.sqrt(HD)
MESH = pl.DeviceIdType.MESH
F32 = jnp.float32
BF16 = jnp.bfloat16
Z_ORDER = (0, -1, 1, -2, 2, -3, 3, -4)


def rms_rows(values, gain):
    factor = lax.rsqrt(jnp.mean(values * values, axis=-1, keepdims=True) + 1e-06)
    return (values * factor * gain).astype(BF16)


def dot_t(a, b):
    return lax.dot_general(a, b, (((1,), (1,)), ((), ())), preferred_element_type=F32)


def dot(a, b):
    return jnp.dot(a, b, preferred_element_type=F32)


def kernel(
    x_hbm, meta_hbm, low_ref, gain_ref, wq_ref, wlow_ref, wout_ref, out_hbm,
    xp, kv, qc, oc, part, pr, fa, fb, r1, r2, res, meta_v, meta_s,
    s_a, r_a, l_a, s_b, r_b, s_z, r_z, s_x, r_x, s_xf, r_xf,
    s_o, r_o, s_ret, r_ret, l_ret, s_m, r_m, l_m,
):
    t = lax.axis_index("tok")
    h = lax.axis_index("head")
    x, z = t // NZ, lax.rem(t, NZ)
    y, c = h // 2, lax.rem(h, 2)
    v, q4 = t // 4, lax.rem(t, 4)

    def view_dev(s):
        return {"head": h, "tok": lax.rem(v + s, VIEWS) * 4 + q4}

    def y_of(d):
        return lax.rem(y + d + NY, NY)

    def y_dev(d):
        return {"head": y_of(d) * 2 + c, "tok": t}

    def z_of(d):
        return lax.rem(z + d + NZ, NZ)

    def x_of(d):
        return lax.rem(x + d + 4, 4)

    partner = {"head": y * 2 + 1 - c, "tok": t}
    y_up, y_dn = y_dev(1), y_dev(-1)
    z_up = {"head": h, "tok": x * NZ + z_of(1)}
    z_dn = {"head": h, "tok": x * NZ + z_of(-1)}
    x_up = {"head": h, "tok": x_of(1) * NZ + z}
    x_dn = {"head": h, "tok": x_of(-1) * NZ + z}

    def remote(src, dst, ss, rs, dev):
        return pltpu.make_async_remote_copy(
            src_ref=src, dst_ref=dst, send_sem=ss, recv_sem=rs, device_id=dev, device_id_type=MESH
        )

    def wait_bytes(ref, sem):
        pltpu.make_async_copy(ref, ref, sem).wait()

    barrier = pltpu.get_barrier_semaphore()
    peers = [view_dev(s) for s in range(1, VIEWS)] + [partner, y_up, y_dn, z_up, z_dn]
    for dev in peers:
        pl.semaphore_signal(barrier, inc=1, device_id=dev, device_id_type=MESH)
    pl.semaphore_wait(barrier, len(peers))

    def rows_start(k):
        for s in range(1, VIEWS):
            remote(
                x_hbm.at[lax.rem(v + s, VIEWS), k, h], xp.at[k, h, VIEWS - s],
                s_a.at[k], r_a.at[k], view_dev(s),
            ).start()
        pltpu.make_async_copy(x_hbm.at[v, k], xp.at[k, :, 0], l_a.at[k]).start()

    def piece(k, d, other=False):
        return xp.at[k, y_of(d) * 2 + (1 - c if other else c), pl.ds(1, VIEWS - 1)]

    def half(k, d, part_index):
        return xp.at[k, y_of(d) * 2 + c, pl.ds(1, VIEWS - 1), :, pl.ds(part_index * 512, 512)]

    def share(k, slot, ref, dev):
        return remote(ref, ref, s_b.at[k, slot], r_b.at[k, slot], dev)

    def in_a(k):
        wait_bytes(piece(k, 0), r_a.at[k])
        share(k, 0, piece(k, 0), y_up).start()
        share(k, 1, piece(k, 0), y_dn).start()
        share(k, 4, piece(k, 0), partner).start()

    def in_b(k):
        wait_bytes(piece(k, -1), r_b.at[k, 0])
        share(k, 2, half(k, -1, 0), y_up).start()
        share(k, 5, piece(k, -1), partner).start()
        wait_bytes(piece(k, 1), r_b.at[k, 1])
        share(k, 3, half(k, 1, 1), y_dn).start()
        share(k, 6, piece(k, 1), partner).start()

    def in_c(k):
        wait_bytes(half(k, 2, 0), r_b.at[k, 2])
        wait_bytes(half(k, 2, 1), r_b.at[k, 3])
        share(k, 7, piece(k, 2), partner).start()

    def in_d(k):
        for slot, d in ((4, 0), (5, -1), (6, 1), (7, 2)):
            wait_bytes(piece(k, d, True), r_b.at[k, slot])
        wait_bytes(xp.at[k, :, 0], l_a.at[k])

    def in_sends(k):
        wait_bytes(piece(k, 0), s_a.at[k])
        for slot, ref in (
            (0, piece(k, 0)), (1, piece(k, 0)), (2, half(k, -1, 0)), (3, half(k, 1, 1)),
            (4, piece(k, 0)), (5, piece(k, -1)), (6, piece(k, 1)), (7, piece(k, 2)),
        ):
            wait_bytes(ref, s_b.at[k, slot])

    def kv_block(dx, dz):
        return kv.at[pl.ds((x_of(dx) * NZ + z_of(dz)) * 2, 2)]

    def kv_half(dx, dz, part_index):
        return kv.at[(x_of(dx) * NZ + z_of(dz)) * 2 + part_index]

    def kv_z(i, dz, dev):
        return remote(kv_block(0, dz), kv_block(0, dz), s_z.at[i], r_z.at[i], dev)

    def kv_x_start(i):
        ref = kv_block(0, Z_ORDER[i])
        remote(ref, ref, s_x.at[i, 0], r_x.at[i, 0], x_up).start()
        remote(ref, ref, s_x.at[i, 1], r_x.at[i, 1], x_dn).start()

    def kv_x_forward(i):
        dz = Z_ORDER[i]
        wait_bytes(kv_block(-1, dz), r_x.at[i, 0])
        ref = kv_half(-1, dz, 0)
        remote(ref, ref, s_xf.at[i, 0], r_xf.at[i, 0], x_up).start()
        wait_bytes(kv_block(1, dz), r_x.at[i, 1])
        ref = kv_half(1, dz, 1)
        remote(ref, ref, s_xf.at[i, 1], r_xf.at[i, 1], x_dn).start()

    def kv_z_step(i):
        dz = Z_ORDER[i]
        wait_bytes(kv_block(0, dz), r_z.at[i])
        if i + 2 < VIEWS:
            kv_z(i + 2, dz, z_up if dz < 0 else z_dn).start()
        kv_x_start(i)

    def kv_last():
        for i, dz in enumerate(Z_ORDER):
            wait_bytes(kv_half(2, dz, 0), r_xf.at[i, 0])
            wait_bytes(kv_half(2, dz, 1), r_xf.at[i, 1])

    def kv_sends():
        for i, dz in enumerate(Z_ORDER):
            if i:
                wait_bytes(kv_block(0, dz), s_z.at[i])
            for e in range(2):
                wait_bytes(kv_block(0, dz), s_x.at[i, e])
                wait_bytes(kv_half(0, dz, 0), s_xf.at[i, e])

    for s in range(1, VIEWS):
        remote(
            meta_hbm.at[lax.rem(v + s, VIEWS)], meta_v.at[VIEWS - s], s_m, r_m, view_dev(s)
        ).start()
    pltpu.make_async_copy(meta_hbm.at[v], meta_v.at[0], l_m).start()

    rows_start(0)
    low = rms_rows(low_ref[...].astype(F32), gain_ref[...])
    kv[pl.ds(t * 2, 2)] = dot(low, wlow_ref[...]).astype(BF16).reshape(2, HD, 2 * HD)
    kv_z(1, 0, z_up).start()
    kv_z(2, 0, z_dn).start()
    kv_x_start(0)
    rows_start(1)

    row = lax.broadcasted_iota(jnp.int32, (HD, HD), 0)
    col = lax.broadcasted_iota(jnp.int32, (HD, HD), 1)
    same_pixel = jnp.where(lax.rem(row, PIECE) == lax.rem(col, PIECE), 0.0, MASKED).astype(F32)

    def project(k):
        def body(r, carry):
            rows = xp[k, pl.ds(r * 2, 2)].reshape(2 * HD, HEADS * HD).astype(F32)
            both = dot(rms_rows(rows, gain_ref[...]), wq_ref[...])
            scaled = jnp.concatenate([both[:, : 2 * HD] * SCORE_SCALE, both[:, 2 * HD :]], axis=1)
            qc[pl.ds(r * 2, 2)] = scaled.astype(BF16).reshape(2, VIEWS, PIECE, 4 * HD)
            return carry

        lax.fori_loop(0, HEADS // 2, body, 0)

    def view_attend():
        def body(g, carry):
            rows = qc[g].reshape(HD, 4 * HD)
            scores = dot_t(rows[:, HD : 2 * HD], rows[:, 2 * HD : 3 * HD]) + same_pixel
            weights = jnp.exp2(scores - jnp.max(scores, axis=-1, keepdims=True))
            total = jnp.sum(weights, axis=-1, keepdims=True)
            mixed = dot(weights.astype(BF16), rows[:, 3 * HD :]) / total
            oc[:, pl.ds(g * PIECE, PIECE), HD:] = mixed.astype(BF16).reshape(VIEWS, PIECE, HD)
            return carry

        lax.fori_loop(0, HEADS, body, 0, unroll=2)

    def cross_attend(k, first, last):
        def body(s, carry):
            queries = qc[:, s, :, :HD].reshape(HD, HD)
            count = meta_s[s, 0, 4 * MAXB + k]
            scores, values = [], []
            for pair in range(MAXB // 2):
                ids = [meta_s[s, 0, k * MAXB + 2 * pair + e] for e in range(2)]
                keys = jnp.concatenate([kv[ids[e], :, :HD] for e in range(2)], axis=0)
                values.append(jnp.concatenate([kv[ids[e], :, HD:] for e in range(2)], axis=0))
                raw = dot_t(queries, keys)
                for e in range(2):
                    bias = jnp.where(2 * pair + e < count, 0.0, MASKED).astype(F32)
                    scores.append(raw[:, e * HD : (e + 1) * HD] + bias)
            top = functools.reduce(jnp.maximum, scores)
            top = jnp.max(top, axis=-1, keepdims=True)
            weights = [jnp.exp2(score - top) for score in scores]
            total = jnp.sum(functools.reduce(jnp.add, weights), axis=-1, keepdims=True)
            mixed = functools.reduce(
                jnp.add,
                [
                    dot(jnp.concatenate(weights[2 * p : 2 * p + 2], axis=1).astype(BF16), values[p])
                    for p in range(MAXB // 2)
                ],
            )
            oc[s, :, :HD] = (mixed / total).astype(BF16)
            return carry

        lax.fori_loop(first, last, body, 0)

    def out_project(k):
        def body(r, carry):
            rows = oc[pl.ds(r * 2, 2)].reshape(2 * HD, 2 * HD)
            summed = dot(rows, wout_ref[...]).astype(BF16)
            for j in range(HEADS):
                part[k, j % 2, j // 2, pl.ds(r * 2 * HD, 2 * HD)] = summed[:, j * HD : (j + 1) * HD]
            return carry

        lax.fori_loop(0, VIEWS // 2, body, 0)

    def core_send(k):
        return remote(part.at[k, 1 - c], pr.at[k], s_o.at[k, 0], r_o.at[k, 0], partner)

    def far_sends(k):
        a = y_of(2)
        return (
            remote(part.at[k, c, a, pl.ds(0, 512)], fa.at[k], s_o.at[k, 1], r_o.at[k, 1], y_up),
            remote(part.at[k, c, a, pl.ds(512, 512)], fb.at[k], s_o.at[k, 2], r_o.at[k, 2], y_dn),
        )

    def near_sends(k):
        return (
            remote(part.at[k, c, y_of(1)], r1.at[k], s_o.at[k, 3], r_o.at[k, 3], y_up),
            remote(part.at[k, c, y_of(-1)], r2.at[k], s_o.at[k, 4], r_o.at[k, 4], y_dn),
        )

    def out_a(k):
        core_send(k).wait_recv()
        a = y_of(2)

        def body(r, carry):
            rows = pl.ds(r * 256, 256)
            part[k, c, a, rows] = (part[k, c, a, rows].astype(F32) + pr[k, a, rows].astype(F32)).astype(BF16)
            return carry

        lax.fori_loop(0, 4, body, 0)
        for copy in far_sends(k):
            copy.start()

    def out_b(k):
        for copy in far_sends(k):
            copy.wait_recv()
        up, dn = y_of(1), y_of(-1)

        def body(r, carry):
            with_far, without = pl.ds(r * 256, 256), pl.ds(512 + r * 256, 256)
            for a, far, w0, w1 in ((up, fa, with_far, without), (dn, fb, without, with_far)):
                part[k, c, a, w0] = (
                    part[k, c, a, w0].astype(F32) + pr[k, a, w0].astype(F32)
                    + far[k, pl.ds(r * 256, 256)].astype(F32)
                ).astype(BF16)
                part[k, c, a, w1] = (part[k, c, a, w1].astype(F32) + pr[k, a, w1].astype(F32)).astype(BF16)
            return carry

        lax.fori_loop(0, 2, body, 0)
        for copy in near_sends(k):
            copy.start()

    def home(k, s):
        return remote(res.at[k, s], out_hbm.at[v, k], s_ret.at[k], r_ret.at[k], view_dev(s))

    def out_c(k):
        for copy in near_sends(k):
            copy.wait_recv()

        def body(s, carry):
            rows = pl.ds(s * HD, HD)
            total = part[k, c, y, rows].astype(F32) + pr[k, y, rows].astype(F32)
            total = total + r1[k, rows].astype(F32) + r2[k, rows].astype(F32)
            columns = pl.ds(pl.multiple_of(h * HD, HD), HD)
            residual = xp[k, :, s, :, columns].reshape(HD, HD).astype(F32)
            res[k, s] = (residual + total).astype(BF16)
            return carry

        lax.fori_loop(0, VIEWS, body, 0)
        for s in range(1, VIEWS):
            home(k, s).start()
        pltpu.make_async_copy(res.at[k, 0], out_hbm.at[v, k], l_ret.at[k]).start()

    def out_sends(k):
        for copy in (core_send(k),) + far_sends(k) + near_sends(k):
            copy.wait_send()
        wait_bytes(res.at[k, pl.ds(1, VIEWS - 1)], s_ret.at[k])
        wait_bytes(res.at[k, pl.ds(1, VIEWS - 1)], r_ret.at[k])
        wait_bytes(res.at[k, 0], l_ret.at[k])

    kv_z_step(1)
    kv_z_step(2)
    in_a(0)
    rows_start(2)
    kv_z_step(3)
    kv_z_step(4)
    kv_x_forward(0)
    in_b(0)
    rows_start(3)
    kv_z_step(5)
    kv_z_step(6)
    in_c(0)
    kv_z_step(7)
    wait_bytes(meta_v.at[pl.ds(1, VIEWS - 1)], r_m)
    wait_bytes(meta_v.at[0], l_m)
    meta_copy = pltpu.make_async_copy(meta_v, meta_s, l_m)
    meta_copy.start()
    for i in range(1, VIEWS):
        kv_x_forward(i)
    in_d(0)
    meta_copy.wait()

    def step(i, carry):
        kin, kc, ko = i, i - 1, i - 2
        has_in = jnp.logical_and(i > 0, i < CH)
        has_c = jnp.logical_and(i > 0, i <= CH)
        has_o = i > 1

        @pl.when(has_in)
        def _():
            in_a(kin)

        @pl.when(has_c)
        def _():
            project(kc)

        @pl.when(has_in)
        def _():
            in_b(kin)

        @pl.when(has_o)
        def _():
            out_a(ko)

        @pl.when(has_c)
        def _():
            view_attend()

            @pl.when(i == 1)
            def _():
                kv_last()

            cross_attend(kc, 0, 3)

        @pl.when(has_o)
        def _():
            out_b(ko)

        @pl.when(has_in)
        def _():
            in_c(kin)

        @pl.when(has_c)
        def _():
            cross_attend(kc, 3, VIEWS)

        @pl.when(has_o)
        def _():
            out_c(ko)

        @pl.when(has_c)
        def _():
            out_project(kc)
            core_send(kc).start()

        @pl.when(has_in)
        def _():
            in_d(kin)

        return carry

    lax.fori_loop(1, CH + 2, step, 0)

    wait_bytes(meta_v.at[pl.ds(1, VIEWS - 1)], s_m)
    kv_sends()

    def drain(k, carry):
        in_sends(k)
        out_sends(k)
        return carry

    lax.fori_loop(0, CH, drain, 0)


def shards(hires, low, gain, w_cross_q, w_low_kv, w_view_qkv, w_out, lists, counts):
    width = hires.shape[1]
    cols = w_cross_q.shape[1]
    rows = hires.reshape(VIEWS, CH, HEADS, PIECE, width)
    wq = jnp.concatenate([w_cross_q, w_view_qkv.reshape(width, 3 * cols)], axis=1)
    meta = jnp.concatenate([lists.reshape(VIEWS, CH * MAXB), counts.reshape(VIEWS, CH)], axis=1)
    meta = jnp.pad(meta[:, None, :], ((0, 0), (0, 7), (0, HD - CH * MAXB - CH)))
    vmem = pl.BlockSpec(memory_space=pltpu.VMEM)
    hbm = pl.BlockSpec(memory_space=pl.ANY)
    dma = pltpu.SemaphoreType.DMA
    out = pl.pallas_call(
        kernel,
        out_shape=jax.ShapeDtypeStruct((VIEWS, CH, HD, HD), BF16),
        in_specs=[hbm, hbm, vmem, vmem, vmem, vmem, vmem],
        out_specs=hbm,
        scratch_shapes=[
            pltpu.VMEM((CH, HEADS, VIEWS, PIECE, width), BF16),
            pltpu.VMEM((64, HD, 2 * HD), BF16),
            pltpu.VMEM((HEADS, VIEWS, PIECE, 4 * HD), BF16),
            pltpu.VMEM((VIEWS, HD, 2 * HD), BF16),
            pltpu.VMEM((CH, 2, NY, VIEWS * HD, HD), BF16),
            pltpu.VMEM((CH, NY, VIEWS * HD, HD), BF16),
            pltpu.VMEM((CH, 512, HD), BF16),
            pltpu.VMEM((CH, 512, HD), BF16),
            pltpu.VMEM((CH, VIEWS * HD, HD), BF16),
            pltpu.VMEM((CH, VIEWS * HD, HD), BF16),
            pltpu.VMEM((CH, VIEWS, HD, HD), BF16),
            pltpu.VMEM((VIEWS, 8, HD), jnp.int32),
            pltpu.SMEM((VIEWS, 8, HD), jnp.int32),
            dma((CH,)), dma((CH,)), dma((CH,)),
            dma((CH, 8)), dma((CH, 8)),
            dma((8,)), dma((8,)),
            dma((8, 2)), dma((8, 2)),
            dma((8, 2)), dma((8, 2)),
            dma((CH, 5)), dma((CH, 5)),
            dma((CH,)), dma((CH,)), dma((CH,)),
            dma, dma, dma,
        ],
        name="upscaler",
        compiler_params=pltpu.CompilerParams(
            collective_id=0, has_side_effects=True, vmem_limit_bytes=60 * 1024 * 1024
        ),
    )(rows, meta, low, gain.reshape(1, width), wq, w_low_kv.reshape(width, 2 * cols), w_out.reshape(2 * cols, width))
    return out.reshape(hires.shape[0], cols)


def solution(mesh):
    in_specs = (
        P("tok", None),
        P("tok", None),
        P(),
        P(None, "head"),
        P(None, None, "head"),
        P(None, None, "head"),
        P(None, "head", None),
        P("tok", None),
        P("tok"),
    )
    return jax.shard_map(shards, mesh=mesh, in_specs=in_specs, out_specs=P("tok", "head"), check_vma=False)
```

time: 337 us -> 167 us (0.50)
  waiting for transfers between devices: 167 us -> 0 us
  Pallas kernels: 0 us -> 157 us
  local copies, waits for them, and re-layouts: 70.1 us -> 8.19 us
  matrix products: 57.9 us -> 0 us
  starting transfers between devices: 17.2 us -> 0 us
  between operations: 13.6 us -> 0.04 us
  other arithmetic: 9.74 us -> 1.14 us
    pallas_call x0 -> x1, Pallas kernels: none -> 157 us  [shards(): pl.pallas_call(kernel, out_shape=jax.ShapeDtypeStruct((VIEWS, CH, HD, HD)...]
    all_to_all x2 -> x0, waiting for transfers between devices: 111 us -> none  [the longest x1 111 us: shards(): lax.all_to_all(view_qkv, 'tok', split_axis=0, concat_axis=0, tiled=True)]
    dot_general x23 -> x0, matrix products: 57.9 us -> none  [the longest x8 12.6 us: attend_group(): jnp.einsum('gqhe,gkhe->ghqk', queries, picked[:, :, 0], preferred_element...]
    unnamed x3 -> x0, waiting for transfers between devices: 56.2 us -> none
    gather x16 -> x0, local copies, waits for them, and re-layouts: 26.2 us -> none  [attend_group(): low_blocks[block_ids].reshape(group_size, MAXB * BLOCK, 2, heads_here, HD)]
    all_to_all x2 -> x0, starting transfers between devices: 16.9 us -> none  [the longest x1 12.3 us: shards(): lax.all_to_all(view_qkv, 'tok', split_axis=0, concat_axis=0, tiled=True)]
    unnamed x19 -> x6, local copies, waits for them, and re-layouts: 19.5 us -> 6.42 us
    reshape x3, local copies, waits for them, and re-layouts: 11.8 us -> 1.16 us  [the longest x1 0.73 us: shards(): counts.reshape(VIEWS, CH)]
  transfers between devices with their start and end apart: 4 -> 0, of which waited for: 2 -> 0; matrix products, arithmetic and copies ran while one was open for 32% -> 0% of each run, Pallas kernels for 0% -> 0%
where the time goes in v1:
time: 167 us
  Pallas kernels  157 us (94%)
  local copies, waits for them, and re-layouts  8.19 us (5%)
    pallas_call x1, Pallas kernels, shards(): pl.pallas_call(kernel, out_shape=jax.ShapeDtypeStruct((VIEWS, CH, HD, HD)...  157 us
    unnamed x6, local copies, waits for them, and re-layouts  6.42 us

profile of v1, /device:TPU:1, one launch (start us, length us, event | category | flops | bytes accessed | tf_op | source)
XLA Modules:
  0.0 166.7 jit_solution(14315157447062856170)
XLA Ops:
  0.0 0.7 reshape.26
  0.7 0.8 copy.12
  1.5 0.1 reshape.25
  1.6 0.1 pad_add_fusion
  1.6 0.6 pad.4.meta_hbm
  2.3 0.0 copy-start
  2.3 2.0 %copy.17 = bf16[128,8,2,128]{3,1,2,0:T(8,128)(2,1)} copy(bf16[128,8,2,128]{3,2,1,0:T(2,128)(2,1)} %bitcast.15) | data formatting | bytes 1048576
  4.3 1.4 copy.13
  5.7 0.4 copy.14
  6.0 0.0 copy-done
  6.0 1.1 pad_maximum_fusion.wq_ref
  7.1 157.3 %upscaler.1 = bf16[8,4,128,128]{3,2,1,0:T(8,128)(2,1)} custom-call(bf16[8,4,8,16,1024]{4,3,2,1,0:T(8,128)(2,1)} %bitcast.10, s32[8,8,128]{2,1,0:T(8,128)} %pad.4.meta_hbm, bf16[256,1024]{1,0:T(8,128)(2,1)} %low_ref.1, f32[1,1024]{1,0:T(1,128)} %bitcast.17, bf16[1024,512]{1,0:T(8,128)(2,1)} %pad_maximum_fusion.wq_ref, bf16[1024,256]{1,0:T(8,128)(2,1)} %bitcast.13, ...), custom_call_target="tpu_custom_call" | custom-call | tf_op jit(solution)/shard_map/upscaler/pallas_call | solution.py:438
  164.4 2.3 %copy.19 = bf16[4096,128]{1,0:T(8,128)(2,1)} copy(bf16[4096,128]{1,0:T(8,128)(2,1)} %bitcast.11) | data formatting | bytes 2097152
Async XLA Ops:
  2.3 3.8 %copy-start = (bf16[1024,128]{1,0:T(8,128)(2,1)S(1)}, bf16[1024,128]{1,0:T(8,128)(2,1)}, u32[]{:S(2)}) copy-start(bf16[1024,128]{1,0:T(8,128)(2,1)} %param.12) | copy-start | bytes 786436

commit v2 on v1

v2 whole, which is shorter than its diff:
```python
import functools
import math

import jax
import jax.numpy as jnp
from jax import lax
from jax.experimental import pallas as pl
from jax.experimental.pallas import tpu as pltpu
from jax.sharding import PartitionSpec as P

HD = 128
VIEWS = 8
MAXB = 8
NY, NZ = 4, 8
CH = 4
PIECE = 16
HEADS = 8
MASKED = -1e30
SCORE_SCALE = math.log2(math.e) / math.sqrt(HD)
MESH = pl.DeviceIdType.MESH
F32 = jnp.float32
BF16 = jnp.bfloat16
Z_ORDER = (0, -1, 1, -2, 2, -3, 3, -4)
SLOT_VIEW = (0, 2, 4, 6, 1, 3, 5, 7)
GROUPS = ((1, 3), (4, 4))
KV_MAIN = 112


def rms_rows(values, gain):
    factor = lax.rsqrt(jnp.mean(values * values, axis=-1, keepdims=True) + 1e-06)
    return (values * factor * gain).astype(BF16)


def dot_t(a, b):
    return lax.dot_general(a, b, (((1,), (1,)), ((), ())), preferred_element_type=F32)


def dot(a, b):
    return jnp.dot(a, b, preferred_element_type=F32)


def kernel(
    x_hbm, meta_hbm, low_ref, gain_ref, wq_ref, wlow_ref, wout_ref, out_hbm,
    xp, kv, kvb, qc, oc, part, pr, fa, fb, r1, r2, res, meta_v, meta_s,
    s_a, r_a, l_a, s_b, r_b, s_z, r_z, s_x, r_x, s_xf, r_xf, s_h, r_h, s_hz, r_hz,
    s_o, r_o, s_ret, r_ret, l_ret, s_m, r_m, l_m,
):
    t = lax.axis_index("tok")
    h = lax.axis_index("head")
    x, z = t // NZ, lax.rem(t, NZ)
    y, c = h // 2, lax.rem(h, 2)
    v, q4 = t // 4, lax.rem(t, 4)

    def view_dev(s):
        return {"head": h, "tok": lax.rem(v + s, VIEWS) * 4 + q4}

    def y_of(d):
        return lax.rem(y + d + NY, NY)

    def y_dev(d):
        return {"head": y_of(d) * 2 + c, "tok": t}

    def z_of(d):
        return lax.rem(z + d + NZ, NZ)

    def x_of(d):
        return lax.rem(x + d + 4, 4)

    partner = {"head": y * 2 + 1 - c, "tok": t}
    y_up, y_dn = y_dev(1), y_dev(-1)
    z_up = {"head": h, "tok": x * NZ + z_of(1)}
    z_dn = {"head": h, "tok": x * NZ + z_of(-1)}
    x_up = {"head": h, "tok": x_of(1) * NZ + z}
    x_dn = {"head": h, "tok": x_of(-1) * NZ + z}

    def remote(src, dst, ss, rs, dev):
        return pltpu.make_async_remote_copy(
            src_ref=src, dst_ref=dst, send_sem=ss, recv_sem=rs, device_id=dev, device_id_type=MESH
        )

    def wait_bytes(ref, sem):
        pltpu.make_async_copy(ref, ref, sem).wait()

    barrier = pltpu.get_barrier_semaphore()
    peers = [view_dev(s) for s in range(1, VIEWS)] + [partner, y_up, y_dn, z_up, z_dn]
    for dev in peers:
        pl.semaphore_signal(barrier, inc=1, device_id=dev, device_id_type=MESH)
    pl.semaphore_wait(barrier, len(peers))

    def slot_of(s):
        return SLOT_VIEW.index(s % VIEWS)

    def slots(g):
        return pl.ds(*GROUPS[g])

    def rows_start(k, g):
        first, n = GROUPS[g]
        for s in SLOT_VIEW[first : first + n]:
            remote(
                x_hbm.at[lax.rem(v + s, VIEWS), k, h], xp.at[k, h, slot_of(-s)],
                s_a.at[k, g], r_a.at[k, g], view_dev(s),
            ).start()
        if g == 0:
            pltpu.make_async_copy(x_hbm.at[v, k], xp.at[k, :, 0], l_a.at[k]).start()

    def piece(k, g, d, other=False):
        return xp.at[k, y_of(d) * 2 + (1 - c if other else c), slots(g)]

    def share(k, g, slot, ref, dev):
        return remote(ref, ref, s_b.at[k, g, slot], r_b.at[k, g, slot], dev)

    def in_a(k, g):
        own = piece(k, g, 0)
        wait_bytes(own, r_a.at[k, g])
        share(k, g, 0, own, y_up).start()
        share(k, g, 1, own, y_dn).start()
        share(k, g, 3, own, partner).start()

    def in_b(k, g):
        wait_bytes(piece(k, g, -1), r_b.at[k, g, 0])
        if g == 0:
            share(k, g, 2, piece(k, g, -1), y_up).start()
        share(k, g, 4, piece(k, g, -1), partner).start()
        wait_bytes(piece(k, g, 1), r_b.at[k, g, 1])
        if g == 1:
            share(k, g, 2, piece(k, g, 1), y_dn).start()
        share(k, g, 5, piece(k, g, 1), partner).start()

    def in_c(k, g):
        wait_bytes(piece(k, g, 2), r_b.at[k, g, 2])
        share(k, g, 6, piece(k, g, 2), partner).start()

    def in_d(k):
        for g in range(2):
            for slot, d in ((3, 0), (4, -1), (5, 1), (6, 2)):
                wait_bytes(piece(k, g, d, True), r_b.at[k, g, slot])
        wait_bytes(xp.at[k, :, 0], l_a.at[k])

    def in_sends(k):
        for g in range(2):
            wait_bytes(piece(k, g, 0), s_a.at[k, g])
            for slot in range(7):
                wait_bytes(piece(k, g, 0), s_b.at[k, g, slot])

    def kv_block(dx, dz):
        return kv.at[pl.ds((x_of(dx) * NZ + z_of(dz)) * 2, 2)]

    def kv_half(dx, dz, part_index):
        return kv.at[(x_of(dx) * NZ + z_of(dz)) * 2 + part_index]

    def kv_z(i, dz, dev):
        return remote(kv_block(0, dz), kv_block(0, dz), s_z.at[i], r_z.at[i], dev)

    def kv_x_start(i):
        ref = kv_block(0, Z_ORDER[i])
        remote(ref, ref, s_x.at[i, 0], r_x.at[i, 0], x_up).start()
        remote(ref, ref, s_x.at[i, 1], r_x.at[i, 1], x_dn).start()

    def kv_x_forward(i):
        dz = Z_ORDER[i]
        wait_bytes(kv_block(-1, dz), r_x.at[i, 0])
        ref = kv_half(-1, dz, 0)
        remote(ref, ref, s_xf.at[i, 0], r_xf.at[i, 0], x_up).start()
        wait_bytes(kv_block(1, dz), r_x.at[i, 1])
        ref = kv_half(1, dz, 1)
        remote(ref, ref, s_xf.at[i, 1], r_xf.at[i, 1], x_dn).start()

    def kv_z_step(i):
        dz = Z_ORDER[i]
        wait_bytes(kv_block(0, dz), r_z.at[i])
        if i + 2 < VIEWS:
            kv_z(i + 2, dz, z_up if dz < 0 else z_dn).start()
        kv_x_start(i)

    def kvb_x_block(d):
        return kvb.at[pl.ds((z * 4 + x_of(d)) * 2, 2)]

    def kvb_x_half(d, e):
        return kvb.at[(z * 4 + x_of(d)) * 2 + e]

    def kvb_z_block(d):
        return kvb.at[pl.ds(z_of(d) * 8, 8)]

    def kvb_x():
        wait_bytes(kvb_x_block(-1), r_h.at[0])
        remote(kvb_x_half(-1, 0), kvb_x_half(-1, 0), s_h.at[2], r_h.at[2], x_up).start()
        wait_bytes(kvb_x_block(1), r_h.at[1])
        remote(kvb_x_half(1, 1), kvb_x_half(1, 1), s_h.at[3], r_h.at[3], x_dn).start()

    def kvb_z(i, dz, dev):
        return remote(kvb_z_block(dz), kvb_z_block(dz), s_hz.at[i], r_hz.at[i], dev)

    def kvb_xf():
        wait_bytes(kvb_x_half(2, 0), r_h.at[2])
        wait_bytes(kvb_x_half(2, 1), r_h.at[3])
        kvb_z(1, 0, z_up).start()
        kvb_z(2, 0, z_dn).start()

    def kvb_z_step(i):
        dz = Z_ORDER[i]
        wait_bytes(kvb_z_block(dz), r_hz.at[i])
        kvb_z(i + 2, dz, z_up if dz < 0 else z_dn).start()

    def kv_last():
        meta_in()
        for i in (6, 7):
            wait_bytes(kvb_z_block(Z_ORDER[i]), r_hz.at[i])
        for i, dz in enumerate(Z_ORDER):
            wait_bytes(kv_half(2, dz, 0), r_xf.at[i, 0])
            wait_bytes(kv_half(2, dz, 1), r_xf.at[i, 1])

    def kv_sends():
        for e in range(2):
            wait_bytes(kvb_x_block(0), s_h.at[e])
            wait_bytes(kvb_x_half(0, e), s_h.at[2 + e])
        for i in range(1, VIEWS):
            wait_bytes(kvb_z_block(0), s_hz.at[i])
        for i, dz in enumerate(Z_ORDER):
            if i:
                wait_bytes(kv_block(0, dz), s_z.at[i])
            for e in range(2):
                wait_bytes(kv_block(0, dz), s_x.at[i, e])
                wait_bytes(kv_half(0, dz, 0), s_xf.at[i, e])

    for s in range(1, VIEWS):
        remote(
            meta_hbm.at[lax.rem(v + s, VIEWS)], meta_v.at[slot_of(-s)], s_m, r_m, view_dev(s)
        ).start()
    pltpu.make_async_copy(meta_hbm.at[v], meta_v.at[0], l_m).start()

    def low_start():
        low = rms_rows(low_ref[...].astype(F32), gain_ref[...])
        both = dot(low, wlow_ref[...]).astype(BF16).reshape(2, HD, 2 * HD)
        kv[pl.ds(t * 2, 2)] = both[:, :KV_MAIN]
        kvb[pl.ds((z * 4 + x) * 2, 2)] = both[:, KV_MAIN:]
        kv_z(1, 0, z_up).start()
        kv_z(2, 0, z_dn).start()
        for e, dev in ((0, x_up), (1, x_dn)):
            remote(kvb_x_block(0), kvb_x_block(0), s_h.at[e], r_h.at[e], dev).start()
        kv_x_start(0)

    row = lax.broadcasted_iota(jnp.int32, (HD, HD), 0)
    col = lax.broadcasted_iota(jnp.int32, (HD, HD), 1)
    same_pixel = jnp.where(lax.rem(row, PIECE) == lax.rem(col, PIECE), 0.0, MASKED).astype(F32)

    def project(k):
        def body(r, carry):
            rows = xp[k, pl.ds(r * 2, 2)].reshape(2 * HD, HEADS * HD).astype(F32)
            both = dot(rms_rows(rows, gain_ref[...]), wq_ref[...])
            scaled = jnp.concatenate([both[:, : 2 * HD] * SCORE_SCALE, both[:, 2 * HD :]], axis=1)
            qc[k, pl.ds(r * 2, 2)] = scaled.astype(BF16).reshape(2, VIEWS, PIECE, 4 * HD)
            return carry

        lax.fori_loop(0, HEADS // 2, body, 0)

    def view_attend(k):
        def body(g, carry):
            rows = qc[k, g].reshape(HD, 4 * HD)
            scores = dot_t(rows[:, HD : 2 * HD], rows[:, 2 * HD : 3 * HD]) + same_pixel
            weights = jnp.exp2(scores - jnp.max(scores, axis=-1, keepdims=True))
            total = jnp.sum(weights, axis=-1, keepdims=True)
            mixed = dot(weights.astype(BF16), rows[:, 3 * HD :]) / total
            oc[k, :, pl.ds(g * PIECE, PIECE), HD:] = mixed.astype(BF16).reshape(VIEWS, PIECE, HD)
            return carry

        lax.fori_loop(0, HEADS, body, 0, unroll=2)

    def cross_attend(k, u):
        def body(i, carry):
            s = u * 4 + i
            queries = qc[k, :, s, :, :HD].reshape(HD, HD)
            count = meta_s[s, 0, 2 * CH * MAXB + k]
            scores, values = [], []
            for pair in range(MAXB // 2):
                blocks = []
                for e in range(2):
                    at = k * MAXB + 2 * pair + e
                    blocks += [kv[meta_s[s, 0, at]], kvb[meta_s[s, 0, CH * MAXB + at]]]
                both = jnp.concatenate(blocks, axis=0)
                keys = both[:, :HD]
                values.append(both[:, HD:])
                raw = dot_t(queries, keys)
                for e in range(2):
                    bias = jnp.where(2 * pair + e < count, 0.0, MASKED).astype(F32)
                    scores.append(raw[:, e * HD : (e + 1) * HD] + bias)
            top = functools.reduce(jnp.maximum, scores)
            top = jnp.max(top, axis=-1, keepdims=True)
            weights = [jnp.exp2(score - top) for score in scores]
            total = jnp.sum(functools.reduce(jnp.add, weights), axis=-1, keepdims=True)
            mixed = functools.reduce(
                jnp.add,
                [
                    dot(jnp.concatenate(weights[2 * p : 2 * p + 2], axis=1).astype(BF16), values[p])
                    for p in range(MAXB // 2)
                ],
            )
            oc[k, s, :, :HD] = (mixed / total).astype(BF16)
            return carry

        lax.fori_loop(0, 4, body, 0)

    def out_project(k, u):
        def body(r, carry):
            rows = oc[k, pl.ds(u * 4 + r * 2, 2)].reshape(2 * HD, 2 * HD)
            summed = dot(rows, wout_ref[...]).astype(BF16)
            for j in range(HEADS):
                part[k, u, j % 2, j // 2, pl.ds(r * 2 * HD, 2 * HD)] = summed[:, j * HD : (j + 1) * HD]
            return carry

        lax.fori_loop(0, 2, body, 0)
        core_send(k, u).start()

    def core_send(k, u):
        return remote(part.at[k, u, 1 - c], pr.at[k, u], s_o.at[k, u, 0], r_o.at[k, u, 0], partner)

    def far_sends(k, u):
        a = y_of(2)
        return (
            remote(part.at[k, u, c, a, pl.ds(0, 256)], fa.at[k, u], s_o.at[k, u, 1], r_o.at[k, u, 1], y_up),
            remote(part.at[k, u, c, a, pl.ds(256, 256)], fb.at[k, u], s_o.at[k, u, 2], r_o.at[k, u, 2], y_dn),
        )

    def near_sends(k, u):
        return (
            remote(part.at[k, u, c, y_of(1)], r1.at[k, u], s_o.at[k, u, 3], r_o.at[k, u, 3], y_up),
            remote(part.at[k, u, c, y_of(-1)], r2.at[k, u], s_o.at[k, u, 4], r_o.at[k, u, 4], y_dn),
        )

    def add_core(k, u, a, rows):
        return part[k, u, c, a, rows].astype(F32) + pr[k, u, a, rows].astype(F32)

    def out_a(k, u):
        core_send(k, u).wait_recv()
        a = y_of(2)

        def body(r, carry):
            rows = pl.ds(r * 256, 256)
            part[k, u, c, a, rows] = add_core(k, u, a, rows).astype(BF16)
            return carry

        lax.fori_loop(0, 2, body, 0)
        for copy in far_sends(k, u):
            copy.start()

    def out_b(k, u):
        for copy in far_sends(k, u):
            copy.wait_recv()
        up, dn = y_of(1), y_of(-1)

        def body(r, carry):
            w, first, second = pl.ds(r * 128, 128), pl.ds(r * 128, 128), pl.ds(256 + r * 128, 128)
            for a, far, with_far, without in ((up, fa, first, second), (dn, fb, second, first)):
                part[k, u, c, a, with_far] = (add_core(k, u, a, with_far) + far[k, u, w].astype(F32)).astype(BF16)
                part[k, u, c, a, without] = add_core(k, u, a, without).astype(BF16)
            return carry

        lax.fori_loop(0, 2, body, 0)
        for copy in near_sends(k, u):
            copy.start()

    def home_slots(u):
        return range(1, 4) if u == 0 else range(4, VIEWS)

    def home(k, u, p):
        return remote(
            res.at[k, p], out_hbm.at[v, k], s_ret.at[k, u], r_ret.at[k, u], view_dev(SLOT_VIEW[p])
        )

    def out_c(k, u):
        for copy in near_sends(k, u):
            copy.wait_recv()

        def body(i, carry):
            p = u * 4 + i
            rows = pl.ds(i * HD, HD)
            total = add_core(k, u, y, rows) + r1[k, u, rows].astype(F32) + r2[k, u, rows].astype(F32)
            columns = pl.ds(pl.multiple_of(h * HD, HD), HD)
            residual = xp[k, :, p, :, columns].reshape(HD, HD).astype(F32)
            res[k, p] = (residual + total).astype(BF16)
            return carry

        lax.fori_loop(0, 4, body, 0)
        for p in home_slots(u):
            home(k, u, p).start()
        if u == 0:
            pltpu.make_async_copy(res.at[k, 0], out_hbm.at[v, k], l_ret.at[k]).start()

    def out_sends(k):
        for u in range(2):
            for copy in (core_send(k, u),) + far_sends(k, u) + near_sends(k, u):
                copy.wait_send()
            sent = res.at[k, slots(u)]
            wait_bytes(sent, s_ret.at[k, u])
            wait_bytes(sent, r_ret.at[k, u])
        wait_bytes(res.at[k, 0], l_ret.at[k])

    meta_copy = pltpu.make_async_copy(meta_v, meta_s, l_m)

    def meta_in():
        wait_bytes(meta_v.at[pl.ds(1, VIEWS - 1)], r_m)
        wait_bytes(meta_v.at[0], l_m)
        meta_copy.start()
        meta_copy.wait()

    rows_start(0, 1)
    rows_start(3, 0)
    rows_start(2, 0)
    rows_start(0, 0)
    low_start()
    in_a(2, 0)
    in_a(3, 0)
    kvb_x()
    rows_start(2, 1)
    in_a(0, 1)
    rows_start(1, 0)
    kv_z_step(1)
    kv_z_step(2)
    kvb_xf()
    kv_x_forward(0)
    in_a(0, 0)
    rows_start(3, 1)
    in_b(2, 0)
    in_b(0, 1)
    in_a(2, 1)
    kv_z_step(3)
    kv_x_forward(1)
    in_c(0, 1)
    in_a(1, 0)
    kv_x_forward(2)
    in_b(2, 1)
    in_b(0, 0)
    kvb_z_step(1)
    kv_z_step(4)
    kvb_z_step(2)
    in_b(3, 0)
    kv_x_forward(3)
    in_a(3, 1)
    kv_z_step(5)
    in_c(2, 1)
    kv_z_step(6)
    in_c(2, 0)
    rows_start(1, 1)
    kv_x_forward(4)
    in_c(0, 0)
    in_d(2)
    project(2)
    kv_z_step(7)
    in_b(3, 1)
    kvb_z_step(3)
    in_b(1, 0)
    view_attend(2)
    kvb_z_step(4)
    kv_x_forward(5)
    in_c(3, 1)
    kv_x_forward(6)
    in_d(0)
    project(0)
    in_c(3, 0)
    kv_x_forward(7)
    in_c(1, 0)
    kvb_z_step(5)
    in_a(1, 1)
    view_attend(0)
    in_d(3)
    project(3)
    kv_last()
    cross_attend(2, 0)
    out_project(2, 0)
    in_b(1, 1)
    cross_attend(0, 1)
    out_project(0, 1)
    view_attend(3)
    out_a(2, 0)
    cross_attend(2, 1)
    out_a(0, 1)
    out_project(2, 1)
    cross_attend(3, 1)
    out_b(2, 0)
    in_c(1, 1)
    out_project(3, 1)
    out_a(2, 1)
    out_b(0, 1)
    in_d(1)
    project(1)
    view_attend(1)
    out_a(3, 1)
    cross_attend(1, 0)
    cross_attend(3, 0)
    out_b(2, 1)
    out_project(3, 0)
    out_c(0, 1)
    cross_attend(0, 0)
    out_b(3, 1)
    out_project(1, 0)
    out_a(3, 0)
    out_project(0, 0)
    cross_attend(1, 1)
    out_a(1, 0)
    out_project(1, 1)
    out_c(2, 1)
    out_c(3, 1)
    out_a(0, 0)
    out_c(2, 0)
    out_a(1, 1)
    out_b(1, 0)
    out_b(1, 1)
    out_b(0, 0)
    out_b(3, 0)
    out_c(1, 0)
    out_c(1, 1)
    out_c(0, 0)
    out_c(3, 0)

    wait_bytes(meta_v.at[pl.ds(1, VIEWS - 1)], s_m)
    kv_sends()

    def drain(k, carry):
        in_sends(k)
        out_sends(k)
        return carry

    lax.fori_loop(0, CH, drain, 0)


def shards(hires, low, gain, w_cross_q, w_low_kv, w_view_qkv, w_out, lists, counts):
    width = hires.shape[1]
    cols = w_cross_q.shape[1]
    rows = hires.reshape(VIEWS, CH, HEADS, PIECE, width)
    wq = jnp.concatenate([w_cross_q, w_view_qkv.reshape(width, 3 * cols)], axis=1)
    permuted = (lists // 2) % NZ * 8 + (lists // 16) * 2 + lists % 2
    meta = jnp.concatenate(
        [lists.reshape(VIEWS, CH * MAXB), permuted.reshape(VIEWS, CH * MAXB), counts.reshape(VIEWS, CH)], axis=1
    )
    meta = jnp.pad(meta[:, None, :], ((0, 0), (0, 7), (0, HD - 2 * CH * MAXB - CH)))
    vmem = pl.BlockSpec(memory_space=pltpu.VMEM)
    hbm = pl.BlockSpec(memory_space=pl.ANY)
    dma = pltpu.SemaphoreType.DMA
    out = pl.pallas_call(
        kernel,
        out_shape=jax.ShapeDtypeStruct((VIEWS, CH, HD, HD), BF16),
        in_specs=[hbm, hbm, vmem, vmem, vmem, vmem, vmem],
        out_specs=hbm,
        scratch_shapes=[
            pltpu.VMEM((CH, HEADS, VIEWS, PIECE, width), BF16),
            pltpu.VMEM((64, KV_MAIN, 2 * HD), BF16),
            pltpu.VMEM((64, HD - KV_MAIN, 2 * HD), BF16),
            pltpu.VMEM((CH, HEADS, VIEWS, PIECE, 4 * HD), BF16),
            pltpu.VMEM((CH, VIEWS, HD, 2 * HD), BF16),
            pltpu.VMEM((CH, 2, 2, NY, 512, HD), BF16),
            pltpu.VMEM((CH, 2, NY, 512, HD), BF16),
            pltpu.VMEM((CH, 2, 256, HD), BF16),
            pltpu.VMEM((CH, 2, 256, HD), BF16),
            pltpu.VMEM((CH, 2, 512, HD), BF16),
            pltpu.VMEM((CH, 2, 512, HD), BF16),
            pltpu.VMEM((CH, VIEWS, HD, HD), BF16),
            pltpu.VMEM((VIEWS, 8, HD), jnp.int32),
            pltpu.SMEM((VIEWS, 8, HD), jnp.int32),
            dma((CH, 2)), dma((CH, 2)), dma((CH,)),
            dma((CH, 2, 7)), dma((CH, 2, 7)),
            dma((8,)), dma((8,)),
            dma((8, 2)), dma((8, 2)),
            dma((8, 2)), dma((8, 2)),
            dma((4,)), dma((4,)), dma((8,)), dma((8,)),
            dma((CH, 2, 5)), dma((CH, 2, 5)),
            dma((CH, 2)), dma((CH, 2)), dma((CH,)),
            dma, dma, dma,
        ],
        name="upscaler",
        compiler_params=pltpu.CompilerParams(
            collective_id=0, has_side_effects=True, vmem_limit_bytes=60 * 1024 * 1024
        ),
    )(rows, meta, low, gain.reshape(1, width), wq, w_low_kv.reshape(width, 2 * cols), w_out.reshape(2 * cols, width))
    return out.reshape(hires.shape[0], cols)


def solution(mesh):
    in_specs = (
        P("tok", None),
        P("tok", None),
        P(),
        P(None, "head"),
        P(None, None, "head"),
        P(None, None, "head"),
        P(None, "head", None),
        P("tok", None),
        P("tok"),
    )
    return jax.shard_map(shards, mesh=mesh, in_specs=in_specs, out_specs=P("tok", "head"), check_vma=False)
```

time: 167 us -> 128 us (0.77)
  Pallas kernels: 157 us -> 117 us
    pallas_call x1, Pallas kernels: 157 us -> 117 us  [shards(): pl.pallas_call(kernel, out_shape=jax.ShapeDtypeStruct((VIEWS, CH, HD, HD)...]
where the time goes in v2:
time: 128 us; the launch traced here: 127 us
  Pallas kernels  117 us (91%)
  local copies, waits for them, and re-layouts  8.34 us (7%)
  other arithmetic  1.86 us (1%)
    pallas_call x1, Pallas kernels, shards(): pl.pallas_call(kernel, out_shape=jax.ShapeDtypeStruct((VIEWS, CH, HD, HD)...  117 us
    unnamed x6, local copies, waits for them, and re-layouts  6.41 us

profile of v2, /device:TPU:1, one launch (start us, length us, event | category | flops | bytes accessed | tf_op | source)
XLA Modules:
  0.0 127.2 jit_solution(7721201107010121136)
XLA Ops:
  0.0 0.7 reshape.30
  0.7 0.7 fusion.3
  1.4 0.1 copy.14
  1.5 0.1 reshape.29
  1.6 0.8 copy.13
  2.4 0.1 reshape.28
  2.4 0.1 pad_add_fusion
  2.5 0.6 pad.4.meta_hbm
  3.1 0.0 copy-start
  3.1 2.0 %copy.19 = bf16[128,8,2,128]{3,1,2,0:T(8,128)(2,1)} copy(bf16[128,8,2,128]{3,2,1,0:T(2,128)(2,1)} %bitcast.15) | data formatting | bytes 1048576
  5.1 1.4 %copy.15 = bf16[1024,3,128]{0,2,1:T(8,128)(2,1)S(1)} copy(bf16[1024,3,128]{2,0,1:T(8,128)(2,1)} %param.14) | data formatting | bytes 1572864 | tf_op args[5]
  6.5 0.4 copy.16
  6.9 0.0 copy-done
  6.9 1.1 pad_maximum_fusion.wq_ref
  8.0 117.0 %upscaler.1 = bf16[8,4,128,128]{3,2,1,0:T(8,128)(2,1)} custom-call(bf16[8,4,8,16,1024]{4,3,2,1,0:T(8,128)(2,1)} %bitcast.10, s32[8,8,128]{2,1,0:T(8,128)} %pad.4.meta_hbm, bf16[256,1024]{1,0:T(8,128)(2,1)} %low_ref.1, f32[1,1024]{1,0:T(1,128)} %bitcast.17, bf16[1024,512]{1,0:T(8,128)(2,1)} %pad_maximum_fusion.wq_ref, bf16[1024,256]{1,0:T(8,128)(2,1)} %bitcast.13, ...), custom_call_target="tpu_custom_call" | custom-call | tf_op jit(solution)/shard_map/upscaler/pallas_call | solution.py:538
  125.0 2.3 %copy.21 = bf16[4096,128]{1,0:T(8,128)(2,1)} copy(bf16[4096,128]{1,0:T(8,128)(2,1)} %bitcast.11) | data formatting | bytes 2097152
Async XLA Ops:
  3.1 3.8 %copy-start = (bf16[1024,128]{1,0:T(8,128)(2,1)S(1)}, bf16[1024,128]{1,0:T(8,128)(2,1)}, u32[]{:S(2)}) copy-start(bf16[1024,128]{1,0:T(8,128)(2,1)} %param.12) | copy-start | bytes 786436

commit v3 on v2

--- a/solution.py
+++ b/solution.py
@@ -40,10 +40,11 @@
 
 
 def kernel(
-    x_hbm, meta_hbm, low_ref, gain_ref, wq_ref, wlow_ref, wout_ref, out_hbm,
-    xp, kv, kvb, qc, oc, part, pr, fa, fb, r1, r2, res, meta_v, meta_s,
+    x_hbm, lists_hbm, counts_hbm, low_hbm, gain_ref, wcross_hbm, wview_hbm, wlow_hbm, wout_hbm, out_hbm,
+    low_ref, wq_ref, wlow_ref, wout_ref,
+    xp, kv, kvb, qc, oc, part, pr, fa, fb, r1, r2, res, lists_v, counts_v, lists_s, counts_s,
     s_a, r_a, l_a, s_b, r_b, s_z, r_z, s_x, r_x, s_xf, r_xf, s_h, r_h, s_hz, r_hz,
-    s_o, r_o, s_ret, r_ret, l_ret, s_m, r_m, l_m,
+    s_o, r_o, s_ret, r_ret, l_ret, s_m, r_m, l_m, l_w,
 ):
     t = lax.axis_index("tok")
     h = lax.axis_index("head")
@@ -80,6 +81,19 @@
 
     def wait_bytes(ref, sem):
         pltpu.make_async_copy(ref, ref, sem).wait()
+
+    loads = [
+        pltpu.make_async_copy(low_hbm, low_ref, l_w.at[0]),
+        pltpu.make_async_copy(wlow_hbm, wlow_ref, l_w.at[1]),
+        pltpu.make_async_copy(wcross_hbm, wq_ref.at[:, pl.ds(0, HD)], l_w.at[2]),
+    ]
+    for j in range(3):
+        loads.append(
+            pltpu.make_async_copy(wview_hbm.at[j], wq_ref.at[:, pl.ds((j + 1) * HD, HD)], l_w.at[3 + j])
+        )
+    loads.append(pltpu.make_async_copy(wout_hbm, wout_ref, l_w.at[6]))
+    for load in loads:
+        load.start()
 
     barrier = pltpu.get_barrier_semaphore()
     peers = [view_dev(s) for s in range(1, VIEWS)] + [partner, y_up, y_dn, z_up, z_dn]
@@ -202,7 +216,7 @@
         kvb_z(i + 2, dz, z_up if dz < 0 else z_dn).start()
 
     def kv_last():
-        meta_in()
+        lists_in()
         for i in (6, 7):
             wait_bytes(kvb_z_block(Z_ORDER[i]), r_hz.at[i])
         for i, dz in enumerate(Z_ORDER):
@@ -222,13 +236,16 @@
                 wait_bytes(kv_block(0, dz), s_x.at[i, e])
                 wait_bytes(kv_half(0, dz, 0), s_xf.at[i, e])
 
-    for s in range(1, VIEWS):
-        remote(
-            meta_hbm.at[lax.rem(v + s, VIEWS)], meta_v.at[slot_of(-s)], s_m, r_m, view_dev(s)
-        ).start()
-    pltpu.make_async_copy(meta_hbm.at[v], meta_v.at[0], l_m).start()
+    def lists_start():
+        for s in range(1, VIEWS):
+            for e, src, dst in ((0, lists_hbm, lists_v), (1, counts_hbm, counts_v)):
+                remote(src, dst.at[slot_of(-s)], s_m.at[e], r_m.at[e], view_dev(s)).start()
+        pltpu.make_async_copy(lists_hbm, lists_v.at[0], l_m.at[0]).start()
+        pltpu.make_async_copy(counts_hbm, counts_v.at[0], l_m.at[1]).start()
 
     def low_start():
+        loads[0].wait()
+        loads[1].wait()
         low = rms_rows(low_ref[...].astype(F32), gain_ref[...])
         both = dot(low, wlow_ref[...]).astype(BF16).reshape(2, HD, 2 * HD)
         kv[pl.ds(t * 2, 2)] = both[:, :KV_MAIN]
@@ -263,19 +280,21 @@
             oc[k, :, pl.ds(g * PIECE, PIECE), HD:] = mixed.astype(BF16).reshape(VIEWS, PIECE, HD)
             return carry
 
-        lax.fori_loop(0, HEADS, body, 0, unroll=2)
+        lax.fori_loop(0, HEADS, body, 0, unroll=4)
 
     def cross_attend(k, u):
         def body(i, carry):
             s = u * 4 + i
             queries = qc[k, :, s, :, :HD].reshape(HD, HD)
-            count = meta_s[s, 0, 2 * CH * MAXB + k]
+            query_block = v * CH + k
+            count = counts_s[s, 0, query_block]
             scores, values = [], []
             for pair in range(MAXB // 2):
                 blocks = []
                 for e in range(2):
-                    at = k * MAXB + 2 * pair + e
-                    blocks += [kv[meta_s[s, 0, at]], kvb[meta_s[s, 0, CH * MAXB + at]]]
+                    block = lists_s[s, 2 * pair + e, query_block]
+                    by_z = (lax.rem(block // 2, NZ) * 4 + block // (2 * NZ)) * 2 + lax.rem(block, 2)
+                    blocks += [kv[block], kvb[by_z]]
                 both = jnp.concatenate(blocks, axis=0)
                 keys = both[:, :HD]
                 values.append(both[:, HD:])
@@ -297,7 +316,7 @@
             oc[k, s, :, :HD] = (mixed / total).astype(BF16)
             return carry
 
-        lax.fori_loop(0, 4, body, 0)
+        lax.fori_loop(0, 4, body, 0, unroll=4)
 
     def out_project(k, u):
         def body(r, carry):
@@ -394,13 +413,15 @@
             wait_bytes(sent, r_ret.at[k, u])
         wait_bytes(res.at[k, 0], l_ret.at[k])
 
-    meta_copy = pltpu.make_async_copy(meta_v, meta_s, l_m)
-
-    def meta_in():
-        wait_bytes(meta_v.at[pl.ds(1, VIEWS - 1)], r_m)
-        wait_bytes(meta_v.at[0], l_m)
-        meta_copy.start()
-        meta_copy.wait()
+    def lists_in():
+        copies = []
+        for e, rows, scalars in ((0, lists_v, lists_s), (1, counts_v, counts_s)):
+            wait_bytes(rows.at[pl.ds(1, VIEWS - 1)], r_m.at[e])
+            wait_bytes(rows.at[0], l_m.at[e])
+            copies.append(pltpu.make_async_copy(rows, scalars, l_m.at[e]))
+            copies[e].start()
+        for copy in copies:
+            copy.wait()
 
     rows_start(0, 1)
     rows_start(3, 0)
@@ -409,6 +430,7 @@
     low_start()
     in_a(2, 0)
     in_a(3, 0)
+    lists_start()
     kvb_x()
     rows_start(2, 1)
     in_a(0, 1)
@@ -442,6 +464,8 @@
     rows_start(1, 1)
     kv_x_forward(4)
     in_c(0, 0)
+    for load in loads[2:]:
+        load.wait()
     in_d(2)
     project(2)
     kv_z_step(7)
@@ -511,7 +535,8 @@
     out_c(0, 0)
     out_c(3, 0)
 
-    wait_bytes(meta_v.at[pl.ds(1, VIEWS - 1)], s_m)
+    wait_bytes(lists_v.at[pl.ds(1, VIEWS - 1)], s_m.at[0])
+    wait_bytes(counts_v.at[pl.ds(1, VIEWS - 1)], s_m.at[1])
     kv_sends()
 
     def drain(k, carry):
@@ -526,21 +551,19 @@
     width = hires.shape[1]
     cols = w_cross_q.shape[1]
     rows = hires.reshape(VIEWS, CH, HEADS, PIECE, width)
-    wq = jnp.concatenate([w_cross_q, w_view_qkv.reshape(width, 3 * cols)], axis=1)
-    permuted = (lists // 2) % NZ * 8 + (lists // 16) * 2 + lists % 2
-    meta = jnp.concatenate(
-        [lists.reshape(VIEWS, CH * MAXB), permuted.reshape(VIEWS, CH * MAXB), counts.reshape(VIEWS, CH)], axis=1
-    )
-    meta = jnp.pad(meta[:, None, :], ((0, 0), (0, 7), (0, HD - 2 * CH * MAXB - CH)))
     vmem = pl.BlockSpec(memory_space=pltpu.VMEM)
     hbm = pl.BlockSpec(memory_space=pl.ANY)
     dma = pltpu.SemaphoreType.DMA
     out = pl.pallas_call(
         kernel,
         out_shape=jax.ShapeDtypeStruct((VIEWS, CH, HD, HD), BF16),
-        in_specs=[hbm, hbm, vmem, vmem, vmem, vmem, vmem],
+        in_specs=[hbm, hbm, hbm, hbm, vmem, hbm, hbm, hbm, hbm],
         out_specs=hbm,
         scratch_shapes=[
+            pltpu.VMEM(low.shape, BF16),
+            pltpu.VMEM((width, 4 * cols), BF16),
+            pltpu.VMEM((width, 2 * cols), BF16),
+            pltpu.VMEM((2 * cols, width), BF16),
             pltpu.VMEM((CH, HEADS, VIEWS, PIECE, width), BF16),
             pltpu.VMEM((64, KV_MAIN, 2 * HD), BF16),
             pltpu.VMEM((64, HD - KV_MAIN, 2 * HD), BF16),
@@ -553,8 +576,10 @@
             pltpu.VMEM((CH, 2, 512, HD), BF16),
             pltpu.VMEM((CH, 2, 512, HD), BF16),
             pltpu.VMEM((CH, VIEWS, HD, HD), BF16),
-            pltpu.VMEM((VIEWS, 8, HD), jnp.int32),
-            pltpu.SMEM((VIEWS, 8, HD), jnp.int32),
+            pltpu.VMEM((VIEWS, MAXB, 32), jnp.int32),
+            pltpu.VMEM((VIEWS, 1, 32), jnp.int32),
+            pltpu.SMEM((VIEWS, MAXB, 32), jnp.int32),
+            pltpu.SMEM((VIEWS, 1, 32), jnp.int32),
             dma((CH, 2)), dma((CH, 2)), dma((CH,)),
             dma((CH, 2, 7)), dma((CH, 2, 7)),
             dma((8,)), dma((8,)),
@@ -563,13 +588,16 @@
             dma((4,)), dma((4,)), dma((8,)), dma((8,)),
             dma((CH, 2, 5)), dma((CH, 2, 5)),
             dma((CH, 2)), dma((CH, 2)), dma((CH,)),
-            dma, dma, dma,
+            dma((2,)), dma((2,)), dma((2,)), dma((7,)),
         ],
         name="upscaler",
         compiler_params=pltpu.CompilerParams(
             collective_id=0, has_side_effects=True, vmem_limit_bytes=60 * 1024 * 1024
         ),
-    )(rows, meta, low, gain.reshape(1, width), wq, w_low_kv.reshape(width, 2 * cols), w_out.reshape(2 * cols, width))
+    )(
+        rows, lists.T, counts[None, :], low, gain.reshape(1, width), w_cross_q,
+        w_view_qkv.transpose(1, 0, 2), w_low_kv.reshape(width, 2 * cols), w_out.reshape(2 * cols, width),
+    )
     return out.reshape(hires.shape[0], cols)
 
 

time: 128 us -> 116 us (0.906)
  Pallas kernels: 117 us -> 112 us
  local copies, waits for them, and re-layouts: 8.34 us -> 4.18 us
  other arithmetic: 1.86 us -> 0 us
    pallas_call x1, Pallas kernels: 117 us -> 112 us  [shards(): pl.pallas_call(kernel, out_shape=jax.ShapeDtypeStruct((VIEWS, CH, HD, HD)...]
    unnamed x6 -> x2, local copies, waits for them, and re-layouts: 6.41 us -> 4.18 us
where the time goes in v3:
time: 116 us
  Pallas kernels  112 us (97%)
  local copies, waits for them, and re-layouts  4.18 us (4%)
    pallas_call x1, Pallas kernels, shards(): pl.pallas_call(kernel, out_shape=jax.ShapeDtypeStruct((VIEWS, CH, HD, HD)...  112 us
    unnamed x2, local copies, waits for them, and re-layouts  4.18 us

profile of v3, /device:TPU:1, one launch (start us, length us, event | category | flops | bytes accessed | tf_op | source)
XLA Modules:
  0.0 116.2 jit_solution(5288333213650286720)
XLA Ops:
  0.0 1.9 %copy.12 = bf16[128,8,2,128]{3,1,2,0:T(8,128)(2,1)} copy(bf16[128,8,2,128]{3,2,1,0:T(2,128)(2,1)} %bitcast.15) | data formatting | bytes 1048576
  1.9 112.0 %upscaler.1 = bf16[8,4,128,128]{3,2,1,0:T(8,128)(2,1)} custom-call(bf16[8,4,8,16,1024]{4,3,2,1,0:T(8,128)(2,1)} %bitcast.11, s32[8,32]{1,0:T(8,128)} %bitcast.17, s32[1,32]{1,0:T(1,128)} %bitcast.19, bf16[256,1024]{1,0:T(8,128)(2,1)} %low_hbm.1, f32[1,1024]{1,0:T(1,128)} %bitcast.18, bf16[1024,128]{1,0:T(8,128)(2,1)} %wcross_hbm.1, ...), custom_call_target="tpu_custom_call" | custom-call | tf_op jit(solution)/shard_map/upscaler/pallas_call | solution.py:557
  114.0 2.3 %copy.14 = bf16[4096,128]{1,0:T(8,128)(2,1)} copy(bf16[4096,128]{1,0:T(8,128)(2,1)} %bitcast.12) | data formatting | bytes 2097152

commit v4 on v3

--- a/solution.py
+++ b/solution.py
@@ -41,7 +41,7 @@
 
 def kernel(
     x_hbm, lists_hbm, counts_hbm, low_hbm, gain_ref, wcross_hbm, wview_hbm, wlow_hbm, wout_hbm, out_hbm,
-    low_ref, wq_ref, wlow_ref, wout_ref,
+    low_ref, wq_ref, wlow_ref, wlow_f32, wout_ref,
     xp, kv, kvb, qc, oc, part, pr, fa, fb, r1, r2, res, lists_v, counts_v, lists_s, counts_s,
     s_a, r_a, l_a, s_b, r_b, s_z, r_z, s_x, r_x, s_xf, r_xf, s_h, r_h, s_hz, r_hz,
     s_o, r_o, s_ret, r_ret, l_ret, s_m, r_m, l_m, l_w,
@@ -246,8 +246,12 @@
     def low_start():
         loads[0].wait()
         loads[1].wait()
+        wlow_f32[...] = wlow_ref[...].astype(F32)
+        width = low_ref.shape[1]
+        both = [wlow_f32[pl.ds(j, width, stride=2), :].astype(BF16) for j in range(2)]
+        wlow = jnp.concatenate(both, axis=1)
         low = rms_rows(low_ref[...].astype(F32), gain_ref[...])
-        both = dot(low, wlow_ref[...]).astype(BF16).reshape(2, HD, 2 * HD)
+        both = dot(low, wlow).astype(BF16).reshape(2, HD, 2 * HD)
         kv[pl.ds(t * 2, 2)] = both[:, :KV_MAIN]
         kvb[pl.ds((z * 4 + x) * 2, 2)] = both[:, KV_MAIN:]
         kv_z(1, 0, z_up).start()
@@ -562,7 +566,8 @@
         scratch_shapes=[
             pltpu.VMEM(low.shape, BF16),
             pltpu.VMEM((width, 4 * cols), BF16),
-            pltpu.VMEM((width, 2 * cols), BF16),
+            pltpu.VMEM((2 * width, cols), BF16),
+            pltpu.VMEM((2 * width, cols), F32),
             pltpu.VMEM((2 * cols, width), BF16),
             pltpu.VMEM((CH, HEADS, VIEWS, PIECE, width), BF16),
             pltpu.VMEM((64, KV_MAIN, 2 * HD), BF16),
@@ -596,7 +601,7 @@
         ),
     )(
         rows, lists.T, counts[None, :], low, gain.reshape(1, width), w_cross_q,
-        w_view_qkv.transpose(1, 0, 2), w_low_kv.reshape(width, 2 * cols), w_out.reshape(2 * cols, width),
+        w_view_qkv.transpose(1, 0, 2), w_low_kv.reshape(2 * width, cols), w_out.reshape(2 * cols, width),
     )
     return out.reshape(hires.shape[0], cols)
 

time: 116 us -> 114 us (0.983)
  local copies, waits for them, and re-layouts: 4.18 us -> 2.26 us
    unnamed x2 -> x1, local copies, waits for them, and re-layouts: 4.18 us -> 2.26 us
where the time goes in v4:
time: 114 us; the launch traced here: 113 us
  Pallas kernels  111 us (97%)
  local copies, waits for them, and re-layouts  2.26 us (2%)
    pallas_call x1, Pallas kernels, shards(): pl.pallas_call(kernel, out_shape=jax.ShapeDtypeStruct((VIEWS, CH, HD, HD)...  111 us

profile of v4, /device:TPU:1, one launch (start us, length us, event | category | flops | bytes accessed | tf_op | source)
XLA Modules:
  0.0 113.4 jit_solution(3348923356876949842)
XLA Ops:
  0.0 111.1 %upscaler.1 = bf16[8,4,128,128]{3,2,1,0:T(8,128)(2,1)} custom-call(bf16[8,4,8,16,1024]{4,3,2,1,0:T(8,128)(2,1)} %bitcast.8, s32[8,32]{1,0:T(8,128)} %bitcast.13, s32[1,32]{1,0:T(1,128)} %bitcast.15, bf16[256,1024]{1,0:T(8,128)(2,1)} %low_hbm.1, f32[1,1024]{1,0:T(1,128)} %bitcast.14, bf16[1024,128]{1,0:T(8,128)(2,1)} %wcross_hbm.1, ...), custom_call_target="tpu_custom_call" | custom-call | tf_op jit(solution)/shard_map/upscaler/pallas_call | solution.py:561
  111.1 2.3 %copy.11 = bf16[4096,128]{1,0:T(8,128)(2,1)} copy(bf16[4096,128]{1,0:T(8,128)(2,1)} %bitcast.9) | data formatting | bytes 2097152

commit v5 on v4

--- a/solution.py
+++ b/solution.py
@@ -330,7 +330,7 @@
                 part[k, u, j % 2, j // 2, pl.ds(r * 2 * HD, 2 * HD)] = summed[:, j * HD : (j + 1) * HD]
             return carry
 
-        lax.fori_loop(0, 2, body, 0)
+        lax.fori_loop(0, 2, body, 0, unroll=2)
         core_send(k, u).start()
 
     def core_send(k, u):
@@ -361,7 +361,7 @@
             part[k, u, c, a, rows] = add_core(k, u, a, rows).astype(BF16)
             return carry
 
-        lax.fori_loop(0, 2, body, 0)
+        lax.fori_loop(0, 2, body, 0, unroll=2)
         for copy in far_sends(k, u):
             copy.start()
 
@@ -377,7 +377,7 @@
                 part[k, u, c, a, without] = add_core(k, u, a, without).astype(BF16)
             return carry
 
-        lax.fori_loop(0, 2, body, 0)
+        lax.fori_loop(0, 2, body, 0, unroll=2)
         for copy in near_sends(k, u):
             copy.start()
 
@@ -402,7 +402,7 @@
             res[k, p] = (residual + total).astype(BF16)
             return carry
 
-        lax.fori_loop(0, 4, body, 0)
+        lax.fori_loop(0, 4, body, 0, unroll=4)
         for p in home_slots(u):
             home(k, u, p).start()
         if u == 0:

time: 114 us -> 113 us (level)
  no operation moved by 1% of the time
where the time goes in v5:
time: 113 us; the launch traced here: 112 us
  Pallas kernels  110 us (97%)
  local copies, waits for them, and re-layouts  2.26 us (2%)
    pallas_call x1, Pallas kernels, shards(): pl.pallas_call(kernel, out_shape=jax.ShapeDtypeStruct((VIEWS, CH, HD, HD)...  110 us
    unnamed x1, local copies, waits for them, and re-layouts  2.26 us

profile of v5, /device:TPU:1, one launch (start us, length us, event | category | flops | bytes accessed | tf_op | source)
XLA Modules:
  0.0 112.2 jit_solution(9729010630478167890)
XLA Ops:
  0.0 110.0 %upscaler.1 = bf16[8,4,128,128]{3,2,1,0:T(8,128)(2,1)} custom-call(bf16[8,4,8,16,1024]{4,3,2,1,0:T(8,128)(2,1)} %bitcast.8, s32[8,32]{1,0:T(8,128)} %bitcast.13, s32[1,32]{1,0:T(1,128)} %bitcast.15, bf16[256,1024]{1,0:T(8,128)(2,1)} %low_hbm.1, f32[1,1024]{1,0:T(1,128)} %bitcast.14, bf16[1024,128]{1,0:T(8,128)(2,1)} %wcross_hbm.1, ...), custom_call_target="tpu_custom_call" | custom-call | tf_op jit(solution)/shard_map/upscaler/pallas_call | solution.py:561
  110.0 2.3 %copy.11 = bf16[4096,128]{1,0:T(8,128)(2,1)} copy(bf16[4096,128]{1,0:T(8,128)(2,1)} %bitcast.9) | data formatting | bytes 2097152
